TPU v7x, 32 devices: a whole 2x2x4 slice. The times are simulated.
32 devices in a mesh: dp: 8 (over y, x, core), mp: 4 (over z).
Axes of the slice: x: 2, y: 2, z: 4, core: 2. Of those that a mesh axis runs over, the one named last changes fastest.
Arguments:
- token_ids: int32 [8192], P('dp'), may hold values from 0 to 8191
- segment_ids: int32 [8192], P('dp'), may hold values from 0 to 64, as said below
- timesteps: int32 [8], P('dp'), may hold values from 0 to 999
- token_table: bfloat16 [8192, 768], P(None, 'mp'), may hold values from -4.1875 to 4.1875
- time_table: bfloat16 [1000, 768], P(None, 'mp'), may hold values from -4.1875 to 4.1875
- ln1_gain: float32 [768], replicated, may hold values from 0.1 to 1.9
- ln1_bias: float32 [768], replicated, may hold values from -1.8 to 1.8
- w_qkv: bfloat16 [768, 3, 768], P(None, None, 'mp'), may hold values from -0.3125 to 0.3125
- w_out: bfloat16 [768, 768], P('mp'), may hold values from -1.25 to 1.25
- attn_bias: float32 [768], replicated, may hold values from -3 to 3
- ln2_gain: float32 [768], replicated, may hold values from 0.1 to 1.9
- ln2_bias: float32 [768], replicated, may hold values from -1.8 to 1.8
- w_up: bfloat16 [768, 3072], P(None, 'mp'), may hold values from -0.21875 to 0.21875
- w_down: bfloat16 [3072, 768], P('mp'), may hold values from -0.15625 to 0.15625
- mlp_bias: float32 [768], replicated, may hold values from -3 to 3
- cotangent: bfloat16 [8192, 768], P(('dp', 'mp')), may hold values from -6 to 6
Outputs:
- output: bfloat16 [8192, 768], P(('dp', 'mp'))
- input_grad: float32 [8192, 768], P(('dp', 'mp'))
- grad_token_table: float32 [8192, 768], P('dp', 'mp')
- grad_time_table: float32 [1000, 768], replicated
- grad_ln1_gain: float32 [768], replicated
- grad_ln1_bias: float32 [768], replicated
- grad_w_qkv: float32 [768, 3, 768], P('dp', None, 'mp')
- grad_w_out: float32 [768, 768], P('mp', 'dp')
- grad_attn_bias: float32 [768], replicated
- grad_ln2_gain: float32 [768], replicated
- grad_ln2_bias: float32 [768], replicated
- grad_w_up: float32 [768, 3072], P('dp', 'mp')
- grad_w_down: float32 [3072, 768], P('mp', 'dp')
- grad_mlp_bias: float32 [768], replicated
Inputs may be any that keep to these rules, and one draw needn't show every extreme that they name: `segment_ids`: within each sequence of 1024 tokens the ids start at 1 and rise by 0 or 1 from one token to the next; a tail of padding zeros may follow.
All inputs are finite; a program needn't handle non-finite values.
Results may differ from a plain program's by a relative error of at most 0.018.
The roundings to bfloat16 on the way count: a program that leaves them out, or rounds other values in their place, can miss the bound.
Values may be sent and summed in bfloat16 or wider, within the bound.
A program may use at most 128 MiB of HBM per device.

v0:
```python
import jax
import jax.numpy as jnp
from jax import lax
from jax.sharding import PartitionSpec as P

D = 768
HD = 64
L = 1024
QBLK = 512
PRECISE = lax.Precision.HIGHEST


def as_sent(array):
    return jax.tree.map(lambda a: a.astype(jnp.bfloat16) if a.dtype == jnp.float32 else a, array)


def layer_norm(stream, gain, shift):
    average = jnp.mean(stream, axis=-1, keepdims=True)
    centered = stream - average
    variance = jnp.mean(centered * centered, axis=-1, keepdims=True)
    return centered * lax.rsqrt(variance + 1e-05) * gain + shift


def allowed_pairs(seg_query, segments, first_row):
    key_pos = jnp.arange(L)
    query_pos = first_row + jnp.arange(QBLK)
    same_text = seg_query[:, None] == segments[None, :]
    self_or_text = (seg_query[:, None] != 0) | (query_pos[:, None] == key_pos[None, :])
    return same_text & self_or_text


def attend_forward(queries, key_rows, value_rows, segments):
    outputs = []
    log_parts = []
    for block_index in range(L // QBLK):
        first_row = block_index * QBLK
        query_block = queries[first_row : first_row + QBLK]
        allowed = allowed_pairs(segments[first_row : first_row + QBLK], segments, first_row)
        scores = (
            jnp.einsum("qhd,khd->hqk", query_block, key_rows, preferred_element_type=jnp.float32)
            * 0.125
        )
        masked = jnp.where(allowed[None], scores, -1e30)
        highest = jnp.max(masked, axis=-1, keepdims=True)
        exponents = jnp.exp(masked - highest)
        totals = jnp.sum(exponents, axis=-1, keepdims=True)
        weights = (exponents / totals).astype(jnp.bfloat16)
        outputs.append(
            jnp.einsum(
                "hqk,khd->qhd", weights, value_rows, preferred_element_type=jnp.float32
            ).astype(jnp.bfloat16)
        )
        log_parts.append((highest + jnp.log(totals))[..., 0])
    return (jnp.concatenate(outputs, axis=0), jnp.concatenate(log_parts, axis=1))


def attend_backward(queries, key_rows, value_rows, segments, log_sums, grad_heads):
    grad_keys = jnp.zeros(key_rows.shape, jnp.float32)
    grad_values = jnp.zeros(value_rows.shape, jnp.float32)
    grad_queries = []
    for block_index in range(L // QBLK):
        first_row = block_index * QBLK
        query_block = queries[first_row : first_row + QBLK]
        grad_block = grad_heads[first_row : first_row + QBLK]
        allowed = allowed_pairs(segments[first_row : first_row + QBLK], segments, first_row)
        scores = (
            jnp.einsum("qhd,khd->hqk", query_block, key_rows, preferred_element_type=jnp.float32)
            * 0.125
        )
        masked = jnp.where(allowed[None], scores, -1e30)
        probs = jnp.exp(masked - log_sums[:, first_row : first_row + QBLK, None])
        rounded = probs.astype(jnp.bfloat16)
        grad_probs = jnp.einsum(
            "qhd,khd->hqk", grad_block, value_rows, preferred_element_type=jnp.float32
        )
        inner = jnp.sum(probs * grad_probs, axis=-1, keepdims=True)
        grad_scores = (probs * (grad_probs - inner)).astype(jnp.bfloat16)
        grad_queries.append(
            jnp.einsum("hqk,khd->qhd", grad_scores, key_rows, preferred_element_type=jnp.float32)
            * 0.125
        )
        grad_keys = (
            grad_keys
            + jnp.einsum(
                "hqk,qhd->khd", grad_scores, query_block, preferred_element_type=jnp.float32
            )
            * 0.125
        )
        grad_values = grad_values + jnp.einsum(
            "hqk,qhd->khd", rounded, grad_block, preferred_element_type=jnp.float32
        )
    return (
        jnp.concatenate(grad_queries, axis=0).astype(jnp.bfloat16),
        grad_keys.astype(jnp.bfloat16),
        grad_values.astype(jnp.bfloat16),
    )


def block_forward(
    stream_in,
    segment_ids,
    ln1_gain,
    ln1_bias,
    w_qkv,
    w_out,
    attn_bias,
    ln2_gain,
    ln2_bias,
    w_up,
    w_down,
    mlp_bias,
):
    own_rows = stream_in.shape[0]
    normed_one = layer_norm(stream_in, ln1_gain, ln1_bias).astype(jnp.bfloat16)
    gathered_one = lax.all_gather(normed_one, "mp", axis=0, tiled=True)
    tokens_all = gathered_one.shape[0]
    local_width = w_qkv.shape[2]
    heads_local = local_width // HD
    packed = jnp.dot(
        gathered_one, w_qkv.reshape(D, 3 * local_width), preferred_element_type=jnp.float32
    ).astype(jnp.bfloat16)
    packed = packed.reshape(tokens_all // L, L, 3, heads_local, HD)
    queries = packed[:, :, 0]
    key_rows = packed[:, :, 1]
    value_rows = packed[:, :, 2]
    attended, log_sums = lax.map(
        lambda per_seq: attend_forward(per_seq[0], per_seq[1], per_seq[2], per_seq[3]),
        (queries, key_rows, value_rows, segment_ids.reshape(tokens_all // L, L)),
    )
    attended_flat = attended.reshape(tokens_all, local_width)
    attn_rows = lax.psum_scatter(
        jnp.dot(
            lax.slice_in_dim(attended_flat, 0, own_rows * lax.axis_size("mp"), axis=0),
            w_out,
            preferred_element_type=jnp.float32,
        ),
        "mp",
        scatter_dimension=0,
        tiled=True,
    )
    stream_mid = stream_in + attn_rows + attn_bias
    normed_two = layer_norm(stream_mid, ln2_gain, ln2_bias).astype(jnp.bfloat16)
    gathered_two = lax.all_gather(normed_two, "mp", axis=0, tiled=True)
    pre_act = jnp.dot(gathered_two, w_up, preferred_element_type=jnp.float32)
    activation = jax.nn.gelu(pre_act, approximate=True).astype(jnp.bfloat16)
    mlp_rows = lax.psum_scatter(
        jnp.dot(
            lax.slice_in_dim(activation, 0, own_rows * lax.axis_size("mp"), axis=0),
            w_down,
            preferred_element_type=jnp.float32,
        ).astype(jnp.bfloat16),
        "mp",
        scatter_dimension=0,
        tiled=True,
    ).astype(jnp.float32)
    output = stream_mid + mlp_rows + mlp_bias
    saved = (
        stream_mid,
        gathered_one,
        queries,
        key_rows,
        value_rows,
        attended_flat,
        log_sums,
        gathered_two,
        pre_act,
        activation,
    )
    return (output, saved)


def contract_rows(left, right):
    return lax.dot_general(
        left, right, (((0,), (0,)), ((), ())), preferred_element_type=jnp.float32
    )


def contract_cols(left, right):
    return lax.dot_general(
        left, right, (((1,), (1,)), ((), ())), preferred_element_type=jnp.float32
    )


def on_device(
    token_ids,
    segment_ids,
    timesteps,
    token_table,
    time_table,
    ln1_gain,
    ln1_bias,
    w_qkv,
    w_out,
    attn_bias,
    ln2_gain,
    ln2_bias,
    w_up,
    w_down,
    mlp_bias,
    cotangent,
):
    group_size = lax.axis_size("mp")
    member = lax.axis_index("mp")
    tokens_all = token_ids.shape[0]
    own_rows = tokens_all // group_size
    seq_count = timesteps.shape[0]
    local_width = token_table.shape[1]
    step_match = timesteps[:, None] == jnp.arange(time_table.shape[0])[None, :]
    time_rows = jnp.dot(
        step_match.astype(jnp.bfloat16), time_table, preferred_element_type=jnp.float32
    )
    embedded = (
        token_table[token_ids].astype(jnp.float32).reshape(seq_count, L, local_width)
        + time_rows[:, None, :]
    )
    stream_in = lax.all_to_all(
        embedded.reshape(tokens_all, local_width), "mp", split_axis=0, concat_axis=1, tiled=True
    )
    weights = (
        ln1_gain,
        ln1_bias,
        w_qkv,
        w_out,
        attn_bias,
        ln2_gain,
        ln2_bias,
        w_up,
        w_down,
        mlp_bias,
    )
    output, saved = block_forward(stream_in, segment_ids, *weights)
    repeated, saved = block_forward(lax.optimization_barrier(stream_in), segment_ids, *weights)
    (
        stream_mid,
        gathered_one,
        queries,
        key_rows,
        value_rows,
        attended_flat,
        log_sums,
        gathered_two,
        pre_act,
        activation,
    ) = saved
    own_segments = lax.dynamic_slice_in_dim(segment_ids, member * own_rows, own_rows, 0)
    grad_out = cotangent.astype(jnp.float32) * (own_segments != 0).astype(jnp.float32)[:, None]
    grad_mlp_bias = jnp.sum(grad_out, axis=0)
    grad_mlp_all = lax.all_gather(grad_out.astype(jnp.bfloat16), "mp", axis=0, tiled=True)
    grad_w_down = contract_rows(activation, grad_mlp_all)
    grad_act = contract_cols(grad_mlp_all, w_down)
    gelu_back = jax.vjp(lambda inner: jax.nn.gelu(inner, approximate=True), pre_act)[1]
    grad_pre = gelu_back(grad_act)[0].astype(jnp.bfloat16)
    grad_w_up = contract_rows(gathered_two, grad_pre)
    grad_norm_two = lax.psum_scatter(
        contract_cols(
            lax.slice_in_dim(grad_pre, 0, own_rows * lax.axis_size("mp"), axis=0), w_up
        ).astype(jnp.bfloat16),
        "mp",
        scatter_dimension=0,
        tiled=True,
    ).astype(jnp.float32)
    norm_back_two = jax.vjp(layer_norm, stream_mid, ln2_gain, ln2_bias)[1]
    grad_mid_norm, grad_ln2_gain, grad_ln2_bias = norm_back_two(grad_norm_two)
    grad_mid = grad_out + grad_mid_norm
    grad_attn_bias = jnp.sum(grad_mid, axis=0)
    grad_attn_all = lax.all_gather(grad_mid.astype(jnp.bfloat16), "mp", axis=0, tiled=True)
    grad_w_out = contract_rows(attended_flat, grad_attn_all)
    grad_attended = contract_cols(grad_attn_all, w_out).astype(jnp.bfloat16)
    heads_local = local_width // HD
    grad_heads = grad_attended.reshape(seq_count, L, heads_local, HD)
    grad_q, grad_k, grad_v = lax.map(
        lambda per_seq: attend_backward(
            per_seq[0], per_seq[1], per_seq[2], per_seq[3], per_seq[4], per_seq[5]
        ),
        (queries, key_rows, value_rows, segment_ids.reshape(seq_count, L), log_sums, grad_heads),
    )
    grad_packed = jnp.stack((grad_q, grad_k, grad_v), axis=2).reshape(tokens_all, 3 * local_width)
    grad_w_qkv = contract_rows(gathered_one, grad_packed).reshape(D, 3, local_width)
    qkv_flat = w_qkv.reshape(D, 3 * local_width)
    grad_norm_one = lax.psum_scatter(
        contract_cols(grad_packed, qkv_flat).astype(jnp.bfloat16),
        "mp",
        scatter_dimension=0,
        tiled=True,
    ).astype(jnp.float32)
    norm_back_one = jax.vjp(layer_norm, stream_in, ln1_gain, ln1_bias)[1]
    grad_in_norm, grad_ln1_gain, grad_ln1_bias = norm_back_one(grad_norm_one)
    input_grad = grad_mid + grad_in_norm
    grad_columns = lax.all_to_all(
        as_sent(input_grad), "mp", split_axis=1, concat_axis=0, tiled=True
    ).astype(input_grad.dtype)
    grad_token_table = (
        jnp.zeros((token_table.shape[0], local_width), jnp.float32).at[token_ids].add(grad_columns)
    )
    seq_of_row = (member * own_rows + jnp.arange(own_rows)) // L
    seq_onehot = (seq_of_row[:, None] == jnp.arange(seq_count)[None, :]).astype(jnp.float32)
    seq_sums = lax.dot_general(
        seq_onehot,
        input_grad,
        (((0,), (0,)), ((), ())),
        precision=PRECISE,
        preferred_element_type=jnp.float32,
    )
    grad_time_table = lax.dot_general(
        step_match.astype(jnp.float32),
        seq_sums,
        (((0,), (0,)), ((), ())),
        precision=PRECISE,
        preferred_element_type=jnp.float32,
    )
    small_sums = lax.psum(
        (
            grad_time_table,
            grad_ln1_gain,
            grad_ln1_bias,
            grad_attn_bias,
            grad_ln2_gain,
            grad_ln2_bias,
            grad_mlp_bias,
        ),
        ("dp", "mp"),
    )
    sum_qkv, sum_out, sum_up, sum_down, sum_token = (
        lax.psum_scatter(grad_w_qkv, "dp", scatter_dimension=0, tiled=True),
        lax.psum_scatter(grad_w_out, "dp", scatter_dimension=1, tiled=True),
        lax.psum_scatter(grad_w_up, "dp", scatter_dimension=0, tiled=True),
        lax.psum_scatter(grad_w_down, "dp", scatter_dimension=1, tiled=True),
        lax.psum_scatter(grad_token_table, "dp", scatter_dimension=0, tiled=True),
    )
    return (
        output.astype(jnp.bfloat16),
        input_grad,
        sum_token,
        small_sums[0],
        small_sums[1],
        small_sums[2],
        sum_qkv,
        sum_out,
        small_sums[3],
        small_sums[4],
        small_sums[5],
        sum_up,
        sum_down,
        small_sums[6],
    )


def solution(mesh):
    placed = (
        P("dp"),
        P("dp"),
        P("dp"),
        P(None, "mp"),
        P(None, "mp"),
        P(),
        P(),
        P(None, None, "mp"),
        P("mp", None),
        P(),
        P(),
        P(),
        P(None, "mp"),
        P("mp", None),
        P(),
        P(("dp", "mp"), None),
    )
    return jax.shard_map(
        on_device,
        mesh=mesh,
        in_specs=placed,
        out_specs=(
            P(("dp", "mp"), None),
            P(("dp", "mp"), None),
            P("dp", "mp"),
            P(),
            P(),
            P(),
            P("dp", None, "mp"),
            P("mp", "dp"),
            P(),
            P(),
            P(),
            P("dp", "mp"),
            P("mp", "dp"),
            P(),
        ),
        check_vma=False,
    )
```

profile of v0, /device:TPU:0, one launch (start us, length us, event | category | flops | bytes accessed | tf_op | source)
XLA Modules:
  0.0 1000.9 jit_solution(7275968648900086361)
XLA Ops:
  9.9 5.9 copy.54
  15.8 6.2 gather_fusion
  22.6 26.2 %all_to_all.29 = f32[4,256,192]{1,2,0:T(8,128)S(1)} all-to-all(f32[4,256,192]{1,2,0:T(8,128)S(1)} %broadcast_add_fusion), channel_id=1, replica_groups=mesh['dp'=8,'mp'=4] {'mp'}, dimensions={0} | all-to-all | bytes 1572864 | tf_op jit(solution)/shard_map/all_to_all | solution.py:216
  52.8 34.0 %all-gather.13.cloned.1.call-done = bf16[1024,768]{1,0:T(8,128)(2,1)} async-done(((bf16[256,768]{1,0:T(8,128)(2,1)}), bf16[1024,768]{1,0:T(8,128)(2,1)}) %all-gather.13.cloned.1.call-update) | async-done | bytes 1572880 | tf_op jit(solution)/shard_map/all_gather | solution.py:115
  104.4 58.2 %reduce-scatter.17.cloned.1.call-done = f32[256,768]{1,0:T(8,128)} async-done(((f32[1024,768]{1,0:T(8,128)}), f32[256,768]{1,0:T(8,128)}) %reduce-scatter.17.cloned.1.call-update) | async-done | bytes 786448 | tf_op jit(solution)/shard_map/reduce_scatter | solution.py:131
  165.4 36.5 %all-gather.11.cloned.1.call-done = bf16[1024,768]{1,0:T(8,128)(2,1)} async-done(((bf16[256,768]{1,0:T(8,128)(2,1)}), bf16[1024,768]{1,0:T(8,128)(2,1)}) %all-gather.11.cloned.1.call-update) | async-done | bytes 1572880 | tf_op jit(solution)/shard_map/all_gather | solution.py:248
  201.9 4.8 fusion.134
  206.7 33.2 %all-gather.15.cloned.1.call-done = bf16[1024,768]{1,0:T(8,128)(2,1)} async-done(((bf16[256,768]{1,0:T(8,128)(2,1)}), bf16[1024,768]{1,0:T(8,128)(2,1)}) %all-gather.15.cloned.1.call-update) | async-done | bytes 1572880 | tf_op jit(solution)/shard_map/all_gather | solution.py:143
  239.9 6.5 fusion.16
  250.3 34.3 %reduce-scatter.19.cloned.1.call-done = bf16[256,768]{1,0:T(8,128)(2,1)} async-done(((bf16[1024,768]{1,0:T(8,128)(2,1)}), bf16[256,768]{1,0:T(8,128)(2,1)}) %reduce-scatter.19.cloned.1.call-update) | async-done | bytes 393232 | tf_op jit(solution)/shard_map/reduce_scatter | solution.py:254
  293.0 34.7 %all-gather.17.cloned.1.call-done = bf16[1024,768]{1,0:T(8,128)(2,1)} async-done(((bf16[256,768]{1,0:T(8,128)(2,1)}), bf16[1024,768]{1,0:T(8,128)(2,1)}) %all-gather.17.cloned.1.call-update) | async-done | bytes 1572880 | tf_op jit(solution)/shard_map/all_gather | solution.py:266
  351.4 31.9 %reduce-scatter.21.cloned.1.call-done = bf16[256,768]{1,0:T(8,128)(2,1)} async-done(((bf16[1024,768]{1,0:T(8,128)(2,1)}), bf16[256,768]{1,0:T(8,128)(2,1)}) %reduce-scatter.21.cloned.1.call-update) | async-done | bytes 393232 | tf_op jit(solution)/shard_map/reduce_scatter | solution.py:280
  391.0 35.7 %all-gather.7.cloned.1.call-done = bf16[1024,768]{1,0:T(8,128)(2,1)} async-done(((bf16[256,768]{1,0:T(8,128)(2,1)}), bf16[1024,768]{1,0:T(8,128)(2,1)}) %all-gather.7.cloned.1.call-update) | async-done | bytes 1572880 | tf_op jit(solution)/shard_map/all_gather | solution.py:115
  430.5 6.0 fusion.128
  436.5 6.0 fusion.129
  442.6 4.2 fusion.76
  451.9 59.2 %reduce-scatter.13.cloned.1.call-done = f32[256,768]{1,0:T(8,128)} async-done(((f32[1024,768]{1,0:T(8,128)}), f32[256,768]{1,0:T(8,128)}) %reduce-scatter.13.cloned.1.call-update) | async-done | bytes 786448 | tf_op jit(solution)/shard_map/reduce_scatter | solution.py:131
  517.0 25.0 %all_to_all.30 = bf16[256,4,192]{0,2,1:T(8,128)(2,1)S(1)} all-to-all(bf16[256,4,192]{0,2,1:T(8,128)(2,1)S(1)} %bitcast.201), channel_id=1, replica_groups=mesh['dp'=8,'mp'=4] {'mp'}, dimensions={1} | all-to-all | bytes 786432 | tf_op jit(solution)/shard_map/all_to_all | solution.py:289
  543.4 10.3 %scatter_custom_fusion = f32[8192,192]{1,0:T(8,128)} fusion(s32[1024]{0:T(1024)} %get-tuple-element.151, f32[1024,192]{1,0:T(8,128)} %bitcast.204, f32[]{:T(128)} %constant.117.clone.1), kind=kCustom, calls=%fused_computation.31 | custom fusion | flops 196608 | bytes 6291968 | tf_op jit(solution)/shard_map/scatter-add | solution.py:293
  553.8 4.4 all-gather.9.cloned.1.call-done
  558.2 5.8 convolution_convert_fusion.2
  564.0 5.1 fusion.45
  569.1 4.8 fusion.136
  574.1 4.7 fusion.47
  581.4 14.4 %reduce-scatter.31.cloned.1.call-done = f32[96,192]{1,0:T(8,128)} async-done(((f32[768,192]{1,0:T(8,128)}), f32[96,192]{1,0:T(8,128)}) %reduce-scatter.31.cloned.1.call-update) | async-done | bytes 73744
  597.6 40.3 %all-reduce = (f32[768]{0:T(1024)}, f32[768]{0:T(1024)}, f32[768]{0:T(1024)}, f32[768]{0:T(1024)}, f32[768]{0:T(1024)}, /*index=5*/f32[768]{0:T(1024)}) all-reduce(f32[768]{0:T(1024)S(1)} %copy-done.35, f32[768]{0:T(1024)S(1)} %copy-done.34, f32[768]{0:T(1024)S(1)} %copy-done.32, ...), channel_id=1, replica_groups=mesh['dp'=8,'mp'=4] {'dp','mp'}, use_global_device_ids=true, to_apply=%region_31.32 | all-reduce | flops 4608 | bytes 36864 | tf_op jit(solution)/shard_map/psum | solution.py:311
  637.9 33.2 %reduce-scatter.23.cloned.1.call-done = f32[1024,192]{1,0:T(8,128)} async-done(((f32[8192,192]{1,0:T(8,128)}), f32[1024,192]{1,0:T(8,128)}) %reduce-scatter.23.cloned.1.call-update) | async-done | bytes 786448 | tf_op jit(solution)/shard_map/reduce_scatter | solution.py:328
  673.6 35.3 %reduce-scatter.15.cloned.1.call-done = bf16[256,768]{1,0:T(8,128)(2,1)} async-done(((bf16[1024,768]{1,0:T(8,128)(2,1)}), bf16[256,768]{1,0:T(8,128)(2,1)}) %reduce-scatter.15.cloned.1.call-update) | async-done | bytes 393232 | tf_op jit(solution)/shard_map/reduce_scatter | solution.py:146
  710.7 43.8 %reduce-scatter.29.cloned.1.call-done = f32[768,96]{0,1:T(8,128)} async-done(((f32[768,768]{0,1:T(8,128)}), f32[768,96]{0,1:T(8,128)}) %reduce-scatter.29.cloned.1.call-update) | async-done | bytes 294928 | tf_op jit(solution)/shard_map/reduce_scatter | solution.py:327
  754.5 46.3 %reduce-scatter.27.cloned.1.call-done = f32[96,768]{1,0:T(8,128)} async-done(((f32[768,768]{1,0:T(8,128)}), f32[96,768]{1,0:T(8,128)}) %reduce-scatter.27.cloned.1.call-update) | async-done | bytes 294928 | tf_op jit(solution)/shard_map/reduce_scatter | solution.py:326
  800.8 46.7 %reduce-scatter.25.cloned.1.call-done = f32[96,3,192]{2,0,1:T(8,128)} async-done(((f32[768,3,192]{2,0,1:T(8,128)}), f32[96,3,192]{2,0,1:T(8,128)}) %reduce-scatter.25.cloned.1.call-update) | async-done | bytes 221200 | tf_op jit(solution)/shard_map/reduce_scatter | solution.py:324
  847.5 143.0 %all-reduce.3.cloned.1.call-done = f32[1000,768]{1,0:T(8,128)} async-done(((f32[1000,768]{1,0:T(8,128)}), f32[1000,768]{1,0:T(8,128)}) %all-reduce.3.cloned.1.call-update) | async-done | bytes 3072016 | tf_op jit(solution)/shard_map/psum | solution.py:311
  (215 shorter events, 98.5 us)
Async XLA Ops:
  7.2 232.7 %copy-start = (bf16[768,768]{1,0:T(8,128)(2,1)S(1)}, bf16[768,768]{1,0:T(8,128)(2,1)}, u32[]{:S(2)}) copy-start(bf16[768,768]{1,0:T(8,128)(2,1)} %param.28) | copy-start | bytes 3538948
  7.2 79.6 %all-gather.13.cloned.1.call-start = ((), (), s32[]{:S(2)}) async-start(), calls=%async_computation.17 | async-start | bytes 1966080 | tf_op jit(solution)/shard_map/all_gather | solution.py:115
  22.4 27.0 %copy-start.19 = (f32[768]{0:T(1024)S(1)}, f32[768]{0:T(1024)}, u32[]{:S(2)}) copy-start(f32[768]{0:T(1024)} %param.21) | copy-start | bytes 9220
  22.4 27.0 %copy-start.36 = (f32[768]{0:T(1024)S(1)}, f32[768]{0:T(1024)}, u32[]{:S(2)}) copy-start(f32[768]{0:T(1024)} %param.22) | copy-start | bytes 9220
  22.6 28.1 %copy-start.20 = (s32[1024]{0:T(1024)S(1)}, s32[1024]{0:T(1024)}, u32[]{:S(2)}) copy-start(s32[1024]{0:T(1024)} %param.17) | copy-start | bytes 12292
  50.5 112.1 %reduce-scatter.17.cloned.1.call-start = ((), (), s32[]{:S(2)}) async-start(), calls=%async_computation.18 | async-start | bytes 3932160 | tf_op jit(solution)/shard_map/reduce_scatter | solution.py:131
  52.8 42.5 %copy-start.13 = (pred[512,1024]{1,0:T(8,128)(4,1)}, pred[512,1024]{1,0:T(8,128)(4,1)S(1)}, u32[]{:S(2)}) copy-start(pred[512,1024]{1,0:T(8,128)(4,1)S(1)} %get-tuple-element.153) | copy-start | bytes 1572868
  101.0 61.6 %copy-start.25 = (f32[768]{0:T(1024)S(1)}, f32[768]{0:T(1024)}, u32[]{:S(2)}) copy-start(f32[768]{0:T(1024)} %param.25) | copy-start | bytes 9220
  103.3 60.9 %copy-start.18 = (f32[768]{0:T(1024)S(1)}, f32[768]{0:T(1024)}, u32[]{:S(2)}) copy-start(f32[768]{0:T(1024)} %param.26) | copy-start | bytes 9220
  103.3 98.6 %all-gather.11.cloned.1.call-start = ((), (), s32[]{:S(2)}) async-start(), calls=%async_computation.16 | async-start | bytes 1966080 | tf_op jit(solution)/shard_map/all_gather | solution.py:248
  104.4 135.5 %all-gather.15.cloned.1.call-start = ((), (), s32[]{:S(2)}) async-start(), calls=%async_computation.19 | async-start | bytes 1966080 | tf_op jit(solution)/shard_map/all_gather | solution.py:143
  164.2 122.3 %copy-start.28 = (f32[256]{0:T(256)}, f32[256]{0:T(256)S(1)}, u32[]{:S(2)}) copy-start(f32[256]{0:T(256)S(1)} %fusion.104) | copy-start | bytes 3076
  165.2 119.4 %reduce-scatter.19.cloned.1.call-start = ((), (), s32[]{:S(2)}) async-start(), calls=%async_computation.20 | async-start | bytes 1966080 | tf_op jit(solution)/shard_map/reduce_scatter | solution.py:254
  250.3 77.4 %all-gather.17.cloned.1.call-start = ((), (), s32[]{:S(2)}) async-start(), calls=%async_computation.21 | async-start | bytes 1966080 | tf_op jit(solution)/shard_map/all_gather | solution.py:266
  291.5 91.8 %reduce-scatter.21.cloned.1.call-start = ((), (), s32[]{:S(2)}) async-start(), calls=%async_computation.22 | async-start | bytes 1966080 | tf_op jit(solution)/shard_map/reduce_scatter | solution.py:280
  349.0 77.7 %all-gather.7.cloned.1.call-start = ((), (), s32[]{:S(2)}) async-start(), calls=%async_computation.12 | async-start | bytes 1966080 | tf_op jit(solution)/shard_map/all_gather | solution.py:115
  390.5 40.0 %copy-start.16 = (pred[512,1024]{1,0:T(8,128)(4,1)S(1)}, pred[512,1024]{1,0:T(8,128)(4,1)}, u32[]{:S(2)}) copy-start(pred[512,1024]{1,0:T(8,128)(4,1)} %get-tuple-element.154) | copy-start | bytes 1572868
  390.5 120.6 %reduce-scatter.13.cloned.1.call-start = ((), (), s32[]{:S(2)}) async-start(), calls=%async_computation.13 | async-start | bytes 3932160 | tf_op jit(solution)/shard_map/reduce_scatter | solution.py:131
  451.8 60.9 %copy-start.27 = (f32[768]{0:T(1024)S(1)}, f32[768]{0:T(1024)}, u32[]{:S(2)}) copy-start(f32[768]{0:T(1024)} %param.27) | copy-start | bytes 9220
  451.9 61.9 %copy-start.4 = (bf16[1024,3,64]{0,2,1:T(8,128)(2,1)S(1)}, bf16[1024,3,64]{0,2,1:T(8,128)(2,1)}, u32[]{:S(2)}) copy-start(bf16[1024,3,64]{0,2,1:T(8,128)(2,1)} %copy-done.3) | copy-start | bytes 1179652
  451.9 106.3 %all-gather.9.cloned.1.call-start = ((), (), s32[]{:S(2)}) async-start(), calls=%async_computation.14 | async-start | bytes 1966080 | tf_op jit(solution)/shard_map/all_gather | solution.py:143
  513.7 82.2 %reduce-scatter.31.cloned.1.call-start = ((), (), s32[]{:S(2)}) async-start(), calls=%async_computation.28 | async-start | bytes 884736
  516.8 154.4 %reduce-scatter.23.cloned.1.call-start = ((), (), s32[]{:S(2)}) async-start(), calls=%async_computation.23 | async-start | bytes 9437184 | tf_op jit(solution)/shard_map/reduce_scatter | solution.py:328
  553.7 155.1 %reduce-scatter.15.cloned.1.call-start = ((), (), s32[]{:S(2)}) async-start(), calls=%async_computation.15 | async-start | bytes 1966080 | tf_op jit(solution)/shard_map/reduce_scatter | solution.py:146
  564.0 190.5 %reduce-scatter.29.cloned.1.call-start = ((), (), s32[]{:S(2)}) async-start(), calls=%async_computation.27 | async-start | bytes 2654208 | tf_op jit(solution)/shard_map/reduce_scatter | solution.py:327
  569.1 231.7 %reduce-scatter.27.cloned.1.call-start = ((), (), s32[]{:S(2)}) async-start(), calls=%async_computation.26 | async-start | bytes 2654208 | tf_op jit(solution)/shard_map/reduce_scatter | solution.py:326
  574.0 273.4 %reduce-scatter.25.cloned.1.call-start = ((), (), s32[]{:S(2)}) async-start(), calls=%async_computation.25 | async-start | bytes 2654208 | tf_op jit(solution)/shard_map/reduce_scatter | solution.py:324
  578.8 411.6 %all-reduce.3.cloned.1.call-start = ((), (), s32[]{:S(2)}) async-start(), calls=%async_computation.24 | async-start | bytes 6144000 | tf_op jit(solution)/shard_map/psum | solution.py:311
  579.5 18.0 %copy-start.33 = (f32[768]{0:T(1024)S(1)}, f32[768]{0:T(1024)}, u32[]{:S(2)}) copy-start(f32[768]{0:T(1024)} %get-tuple-element.148) | copy-start | bytes 9220
  579.5 18.1 %copy-start.34 = (f32[768]{0:T(1024)S(1)}, f32[768]{0:T(1024)}, u32[]{:S(2)}) copy-start(f32[768]{0:T(1024)} %get-tuple-element.131) | copy-start | bytes 9220
  579.5 18.1 %copy-start.35 = (f32[768]{0:T(1024)S(1)}, f32[768]{0:T(1024)}, u32[]{:S(2)}) copy-start(f32[768]{0:T(1024)} %get-tuple-element.127) | copy-start | bytes 9220
  581.4 127.4 %copy-start.38 = (f32[768]{0:T(1024)S(1)}, f32[768]{0:T(1024)}, u32[]{:S(2)}) copy-start(f32[768]{0:T(1024)} %param.30) | copy-start | bytes 9220
  (32 other events, 150.1 us)
Sparse Core Ops, SparseCore 0:
  50.6 36.1 all-gather.12
  103.5 59.0 reduce-scatter.16
  164.7 37.1 all-gather.10
  203.9 35.9 all-gather.14
  250.4 34.1 reduce-scatter.18
  291.6 36.0 all-gather.16
  349.1 34.1 reduce-scatter.20
  390.6 36.0 all-gather.6
  452.0 59.0 reduce-scatter.12
  513.8 44.3 all-gather.8
  561.9 33.9 reduce-scatter.30
  599.2 71.8 reduce-scatter.22
  673.5 35.2 reduce-scatter.14
  713.0 41.4 reduce-scatter.28
  758.3 42.4 reduce-scatter.26
  804.9 42.4 reduce-scatter.24
  853.4 137.0 all-reduce.2
where the time goes:
time: 1000 us
  waiting for transfers between devices  725 us (72%)
  blocking collectives  91.6 us (9%)
  matrix products  89.9 us (9%)
  other arithmetic  48.9 us (5%)
  local copies, waits for them, and re-layouts  28.3 us (3%)
  between operations  15.6 us (2%)
    psum x1, waiting for transfers between devices, on_device(): lax.psum((grad_time_table, grad_ln1_gain, grad_ln1_bias, grad_attn_bias,...  143 us
    reduce_scatter x2, waiting for transfers between devices, block_forward(): lax.psum_scatter(jnp.dot(lax.slice_in_dim(attended_flat, 0, own_rows * la...  117 us
    all_gather x2, waiting for transfers between devices, block_forward(): gathered_one = lax.all_gather(normed_one, 'mp', axis=0, tiled=True)  69.7 us
    reduce_scatter x1, waiting for transfers between devices, on_device(): lax.psum_scatter(grad_w_qkv, 'dp', scatter_dimension=0, tiled=True)  46.7 us
    reduce_scatter x1, waiting for transfers between devices, on_device(): lax.psum_scatter(grad_w_up, 'dp', scatter_dimension=0, tiled=True)  46.3 us
    reduce_scatter x1, waiting for transfers between devices, on_device(): lax.psum_scatter(grad_w_down, 'dp', scatter_dimension=1, tiled=True)  43.8 us
    psum x1, blocking collectives, on_device(): lax.psum((grad_time_table, grad_ln1_gain, grad_ln1_bias, grad_attn_bias,...  40.3 us
    all_gather x2, waiting for transfers between devices, block_forward(): gathered_two = lax.all_gather(normed_two, 'mp', axis=0, tiled=True)  37.6 us
  transfers between devices with their start and end apart: 17, of which 17 were waited for; matrix products, arithmetic and copies ran while one was open for 6% of the time, Pallas kernels for 0%

commit v1 on v0

--- a/solution.py
+++ b/solution.py
@@ -309,16 +309,19 @@
         preferred_element_type=jnp.float32,
     )
     small_sums = lax.psum(
-        (
-            grad_time_table,
-            grad_ln1_gain,
-            grad_ln1_bias,
-            grad_attn_bias,
-            grad_ln2_gain,
-            grad_ln2_bias,
-            grad_mlp_bias,
+        lax.psum(
+            (
+                grad_time_table,
+                grad_ln1_gain,
+                grad_ln1_bias,
+                grad_attn_bias,
+                grad_ln2_gain,
+                grad_ln2_bias,
+                grad_mlp_bias,
+            ),
+            "mp",
         ),
-        ("dp", "mp"),
+        "dp",
     )
     sum_qkv, sum_out, sum_up, sum_down, sum_token = (
         lax.psum_scatter(grad_w_qkv, "dp", scatter_dimension=0, tiled=True),

time: 1000 us -> 1060 us (1.060)
  waiting for transfers between devices: 725 us -> 772 us
    psum x0 -> x1, waiting for transfers between devices: none -> 72.6 us  [on_device(): lax.psum(lax.psum((grad_time_table, grad_ln1_gain, grad_ln1_bias, grad_at...]
    psum x1, waiting for transfers between devices: 143 us -> 99.7 us  [on_device(): lax.psum((grad_time_table, grad_ln1_gain, grad_ln1_bias, grad_attn_bias,...]
    psum x0 -> x1, blocking collectives: none -> 23.5 us  [on_device(): lax.psum(lax.psum((grad_time_table, grad_ln1_gain, grad_ln1_bias, grad_at...]
    unnamed x18 -> x19, waiting for transfers between devices: 14.7 us -> 38.2 us
    psum x1, blocking collectives: 40.3 us -> 18.9 us  [on_device(): lax.psum((grad_time_table, grad_ln1_gain, grad_ln1_bias, grad_attn_bias,...]
  transfers between devices with their start and end apart: 17 -> 18, of which waited for: 17 -> 18; matrix products, arithmetic and copies ran while one was open for 6% -> 5% of each run, Pallas kernels for 0% -> 0%
where the time goes in v1:
time: 1060 us; the launch traced here: 1050 us
  waiting for transfers between devices  772 us (73%)
  blocking collectives  95.4 us (9%)
  matrix products  90.2 us (9%)
  other arithmetic  48.9 us (5%)
  local copies, waits for them, and re-layouts  28.2 us (3%)
  between operations  16 us (2%)
    reduce_scatter x2, waiting for transfers between devices, block_forward(): lax.psum_scatter(jnp.dot(lax.slice_in_dim(attended_flat, 0, own_rows * la...  117 us
    psum x1, waiting for transfers between devices, on_device(): lax.psum((grad_time_table, grad_ln1_gain, grad_ln1_bias, grad_attn_bias,...  99.7 us
    psum x1, waiting for transfers between devices, on_device(): lax.psum(lax.psum((grad_time_table, grad_ln1_gain, grad_ln1_bias, grad_at...  72.6 us
    all_gather x2, waiting for transfers between devices, block_forward(): gathered_one = lax.all_gather(normed_one, 'mp', axis=0, tiled=True)  69.7 us
    reduce_scatter x1, waiting for transfers between devices, on_device(): lax.psum_scatter(grad_w_up, 'dp', scatter_dimension=0, tiled=True)  46.7 us
    reduce_scatter x1, waiting for transfers between devices, on_device(): lax.psum_scatter(grad_w_qkv, 'dp', scatter_dimension=0, tiled=True)  46.3 us
    reduce_scatter x1, waiting for transfers between devices, on_device(): lax.psum_scatter(grad_w_down, 'dp', scatter_dimension=1, tiled=True)  43.4 us
    unnamed x19, waiting for transfers between devices  38.2 us
  transfers between devices with their start and end apart: 18, of which 18 were waited for; matrix products, arithmetic and copies ran while one was open for 5% of the time, Pallas kernels for 0%

profile of v1, /device:TPU:0, one launch (start us, length us, event | category | flops | bytes accessed | tf_op | source)
XLA Modules:
  0.0 1052.4 jit_solution(15994189158337968531)
XLA Ops:
  9.9 5.9 copy.54
  15.8 6.2 gather_fusion
  22.6 26.2 %all_to_all.29 = f32[4,256,192]{1,2,0:T(8,128)S(1)} all-to-all(f32[4,256,192]{1,2,0:T(8,128)S(1)} %broadcast_add_fusion), channel_id=1, replica_groups=mesh['dp'=8,'mp'=4] {'mp'}, dimensions={0} | all-to-all | bytes 1572864 | tf_op jit(solution)/shard_map/all_to_all | solution.py:216
  52.8 34.0 %all-gather.13.cloned.1.call-done = bf16[1024,768]{1,0:T(8,128)(2,1)} async-done(((bf16[256,768]{1,0:T(8,128)(2,1)}), bf16[1024,768]{1,0:T(8,128)(2,1)}) %all-gather.13.cloned.1.call-update) | async-done | bytes 1572880 | tf_op jit(solution)/shard_map/all_gather | solution.py:115
  104.5 58.2 %reduce-scatter.17.cloned.1.call-done = f32[256,768]{1,0:T(8,128)} async-done(((f32[1024,768]{1,0:T(8,128)}), f32[256,768]{1,0:T(8,128)}) %reduce-scatter.17.cloned.1.call-update) | async-done | bytes 786448 | tf_op jit(solution)/shard_map/reduce_scatter | solution.py:131
  165.5 36.5 %all-gather.11.cloned.1.call-done = bf16[1024,768]{1,0:T(8,128)(2,1)} async-done(((bf16[256,768]{1,0:T(8,128)(2,1)}), bf16[1024,768]{1,0:T(8,128)(2,1)}) %all-gather.11.cloned.1.call-update) | async-done | bytes 1572880 | tf_op jit(solution)/shard_map/all_gather | solution.py:248
  202.0 4.8 fusion.134
  206.8 33.2 %all-gather.15.cloned.1.call-done = bf16[1024,768]{1,0:T(8,128)(2,1)} async-done(((bf16[256,768]{1,0:T(8,128)(2,1)}), bf16[1024,768]{1,0:T(8,128)(2,1)}) %all-gather.15.cloned.1.call-update) | async-done | bytes 1572880 | tf_op jit(solution)/shard_map/all_gather | solution.py:143
  240.0 6.5 fusion.16
  250.4 34.2 %reduce-scatter.19.cloned.1.call-done = bf16[256,768]{1,0:T(8,128)(2,1)} async-done(((bf16[1024,768]{1,0:T(8,128)(2,1)}), bf16[256,768]{1,0:T(8,128)(2,1)}) %reduce-scatter.19.cloned.1.call-update) | async-done | bytes 393232 | tf_op jit(solution)/shard_map/reduce_scatter | solution.py:254
  293.0 34.7 %all-gather.17.cloned.1.call-done = bf16[1024,768]{1,0:T(8,128)(2,1)} async-done(((bf16[256,768]{1,0:T(8,128)(2,1)}), bf16[1024,768]{1,0:T(8,128)(2,1)}) %all-gather.17.cloned.1.call-update) | async-done | bytes 1572880 | tf_op jit(solution)/shard_map/all_gather | solution.py:266
  351.5 31.9 %reduce-scatter.21.cloned.1.call-done = bf16[256,768]{1,0:T(8,128)(2,1)} async-done(((bf16[1024,768]{1,0:T(8,128)(2,1)}), bf16[256,768]{1,0:T(8,128)(2,1)}) %reduce-scatter.21.cloned.1.call-update) | async-done | bytes 393232 | tf_op jit(solution)/shard_map/reduce_scatter | solution.py:280
  391.1 35.7 %all-gather.7.cloned.1.call-done = bf16[1024,768]{1,0:T(8,128)(2,1)} async-done(((bf16[256,768]{1,0:T(8,128)(2,1)}), bf16[1024,768]{1,0:T(8,128)(2,1)}) %all-gather.7.cloned.1.call-update) | async-done | bytes 1572880 | tf_op jit(solution)/shard_map/all_gather | solution.py:115
  430.6 6.1 fusion.128
  436.6 6.1 fusion.129
  452.1 59.2 %reduce-scatter.13.cloned.1.call-done = f32[256,768]{1,0:T(8,128)} async-done(((f32[1024,768]{1,0:T(8,128)}), f32[256,768]{1,0:T(8,128)}) %reduce-scatter.13.cloned.1.call-update) | async-done | bytes 786448 | tf_op jit(solution)/shard_map/reduce_scatter | solution.py:131
  519.6 26.8 %all_to_all.30 = bf16[256,4,192]{0,2,1:T(8,128)(2,1)S(1)} all-to-all(bf16[256,4,192]{0,2,1:T(8,128)(2,1)S(1)} %bitcast.201), channel_id=1, replica_groups=mesh['dp'=8,'mp'=4] {'mp'}, dimensions={1} | all-to-all | bytes 786432 | tf_op jit(solution)/shard_map/all_to_all | solution.py:289
  547.8 10.3 scatter_custom_fusion
  559.5 5.8 convolution_convert_fusion.2
  565.3 5.6 fusion.45
  571.0 4.9 fusion.136
  576.0 4.3 fusion.47
  580.4 99.7 %all-reduce.5.cloned.1.call-done = f32[1000,768]{1,0:T(8,128)} async-done(((f32[1000,768]{1,0:T(8,128)}), f32[1000,768]{1,0:T(8,128)}) %all-reduce.5.cloned.1.call-update) | async-done | bytes 3072016 | tf_op jit(solution)/shard_map/psum | solution.py:312
  680.1 37.9 %reduce-scatter.31.cloned.1.call-done = f32[96,192]{1,0:T(8,128)} async-done(((f32[768,192]{1,0:T(8,128)}), f32[96,192]{1,0:T(8,128)}) %reduce-scatter.31.cloned.1.call-update) | async-done | bytes 73744
  719.7 18.9 %all-reduce.1 = (f32[768]{0:T(1024)S(1)}, f32[768]{0:T(1024)S(1)}, f32[768]{0:T(1024)S(1)}, f32[768]{0:T(1024)S(1)}, f32[768]{0:T(1024)S(1)}, /*index=5*/f32[768]{0:T(1024)S(1)}) all-reduce(f32[768]{0:T(1024)S(1)} %copy-done.36, f32[768]{0:T(1024)S(1)} %copy-done.35, f32[768]{0:T(1024)S(1)} %copy-done.33, ...), channel_id=1, replica_groups=mesh['dp'=8,'mp'=4] {'mp'}, use_global_device_ids=true, to_apply=%region_32.33 | all-reduce | flops 4608 | bytes 36864 | tf_op jit(solution)/shard_map/psum | solution.py:312
  738.6 23.5 %all-reduce = (f32[768]{0:T(1024)}, f32[768]{0:T(1024)}, f32[768]{0:T(1024)}, f32[768]{0:T(1024)}, f32[768]{0:T(1024)}, /*index=5*/f32[768]{0:T(1024)}) all-reduce(f32[768]{0:T(1024)S(1)} %get-tuple-element.139, f32[768]{0:T(1024)S(1)} %get-tuple-element.140, ...), channel_id=1, replica_groups=mesh['dp'=8,'mp'=4] {'dp'}, use_global_device_ids=true, to_apply=%region_33.34 | all-reduce | flops 4608 | bytes 36864 | tf_op jit(solution)/shard_map/psum | solution.py:311
  762.1 31.3 %reduce-scatter.23.cloned.1.call-done = f32[1024,192]{1,0:T(8,128)} async-done(((f32[8192,192]{1,0:T(8,128)}), f32[1024,192]{1,0:T(8,128)}) %reduce-scatter.23.cloned.1.call-update) | async-done | bytes 786448 | tf_op jit(solution)/shard_map/reduce_scatter | solution.py:331
  795.8 35.1 %reduce-scatter.15.cloned.1.call-done = bf16[256,768]{1,0:T(8,128)(2,1)} async-done(((bf16[1024,768]{1,0:T(8,128)(2,1)}), bf16[256,768]{1,0:T(8,128)(2,1)}) %reduce-scatter.15.cloned.1.call-update) | async-done | bytes 393232 | tf_op jit(solution)/shard_map/reduce_scatter | solution.py:146
  832.7 43.4 %reduce-scatter.29.cloned.1.call-done = f32[768,96]{0,1:T(8,128)} async-done(((f32[768,768]{0,1:T(8,128)}), f32[768,96]{0,1:T(8,128)}) %reduce-scatter.29.cloned.1.call-update) | async-done | bytes 294928 | tf_op jit(solution)/shard_map/reduce_scatter | solution.py:330
  876.1 46.7 %reduce-scatter.27.cloned.1.call-done = f32[96,768]{1,0:T(8,128)} async-done(((f32[768,768]{1,0:T(8,128)}), f32[96,768]{1,0:T(8,128)}) %reduce-scatter.27.cloned.1.call-update) | async-done | bytes 294928 | tf_op jit(solution)/shard_map/reduce_scatter | solution.py:329
  922.8 46.3 %reduce-scatter.25.cloned.1.call-done = f32[96,3,192]{2,0,1:T(8,128)} async-done(((f32[768,3,192]{2,0,1:T(8,128)}), f32[96,3,192]{2,0,1:T(8,128)}) %reduce-scatter.25.cloned.1.call-update) | async-done | bytes 221200 | tf_op jit(solution)/shard_map/reduce_scatter | solution.py:327
  969.1 72.6 %all-reduce.7.cloned.1.call-done = f32[1000,768]{1,0:T(8,128)} async-done(((f32[1000,768]{1,0:T(8,128)}), f32[1000,768]{1,0:T(8,128)}) %all-reduce.7.cloned.1.call-update) | async-done | bytes 3072016 | tf_op jit(solution)/shard_map/psum | solution.py:311
  (221 shorter events, 104.0 us)
Async XLA Ops:
  7.2 232.8 %copy-start = (bf16[768,768]{1,0:T(8,128)(2,1)S(1)}, bf16[768,768]{1,0:T(8,128)(2,1)}, u32[]{:S(2)}) copy-start(bf16[768,768]{1,0:T(8,128)(2,1)} %param.28) | copy-start | bytes 3538948
  7.2 79.6 %all-gather.13.cloned.1.call-start = ((), (), s32[]{:S(2)}) async-start(), calls=%async_computation.17 | async-start | bytes 1966080 | tf_op jit(solution)/shard_map/all_gather | solution.py:115
  50.5 112.2 %reduce-scatter.17.cloned.1.call-start = ((), (), s32[]{:S(2)}) async-start(), calls=%async_computation.18 | async-start | bytes 3932160 | tf_op jit(solution)/shard_map/reduce_scatter | solution.py:131
  101.0 61.7 %copy-start.26 = (f32[768]{0:T(1024)S(1)}, f32[768]{0:T(1024)}, u32[]{:S(2)}) copy-start(f32[768]{0:T(1024)} %param.25) | copy-start | bytes 9220
  103.4 60.9 %copy-start.19 = (f32[768]{0:T(1024)S(1)}, f32[768]{0:T(1024)}, u32[]{:S(2)}) copy-start(f32[768]{0:T(1024)} %param.26) | copy-start | bytes 9220
  103.4 98.6 %all-gather.11.cloned.1.call-start = ((), (), s32[]{:S(2)}) async-start(), calls=%async_computation.16 | async-start | bytes 1966080 | tf_op jit(solution)/shard_map/all_gather | solution.py:248
  104.5 135.5 %all-gather.15.cloned.1.call-start = ((), (), s32[]{:S(2)}) async-start(), calls=%async_computation.19 | async-start | bytes 1966080 | tf_op jit(solution)/shard_map/all_gather | solution.py:143
  164.3 122.3 %copy-start.29 = (f32[256]{0:T(256)}, f32[256]{0:T(256)S(1)}, u32[]{:S(2)}) copy-start(f32[256]{0:T(256)S(1)} %fusion.104) | copy-start | bytes 3076
  165.3 119.4 %reduce-scatter.19.cloned.1.call-start = ((), (), s32[]{:S(2)}) async-start(), calls=%async_computation.20 | async-start | bytes 1966080 | tf_op jit(solution)/shard_map/reduce_scatter | solution.py:254
  250.4 77.4 %all-gather.17.cloned.1.call-start = ((), (), s32[]{:S(2)}) async-start(), calls=%async_computation.21 | async-start | bytes 1966080 | tf_op jit(solution)/shard_map/all_gather | solution.py:266
  291.5 91.8 %reduce-scatter.21.cloned.1.call-start = ((), (), s32[]{:S(2)}) async-start(), calls=%async_computation.22 | async-start | bytes 1966080 | tf_op jit(solution)/shard_map/reduce_scatter | solution.py:280
  349.1 77.7 %all-gather.7.cloned.1.call-start = ((), (), s32[]{:S(2)}) async-start(), calls=%async_computation.12 | async-start | bytes 1966080 | tf_op jit(solution)/shard_map/all_gather | solution.py:115
  390.6 120.7 %reduce-scatter.13.cloned.1.call-start = ((), (), s32[]{:S(2)}) async-start(), calls=%async_computation.13 | async-start | bytes 3932160 | tf_op jit(solution)/shard_map/reduce_scatter | solution.py:131
  452.0 60.9 %copy-start.28 = (f32[768]{0:T(1024)S(1)}, f32[768]{0:T(1024)}, u32[]{:S(2)}) copy-start(f32[768]{0:T(1024)} %param.27) | copy-start | bytes 9220
  452.0 61.9 %copy-start.7 = (f32[256,768]{1,0:T(8,128)S(1)}, f32[256,768]{1,0:T(8,128)}, u32[]{:S(2)}) copy-start(f32[256,768]{1,0:T(8,128)} %get-tuple-element.184) | copy-start | bytes 2359300
  452.0 62.3 %copy-start.30 = (f32[1000]{0:T(1024)S(1)}, f32[1000]{0:T(1024)}, u32[]{:S(2)}) copy-start(f32[1000]{0:T(1024)} %get-tuple-element.182) | copy-start | bytes 12004
  452.0 107.5 %all-gather.9.cloned.1.call-start = ((), (), s32[]{:S(2)}) async-start(), calls=%async_computation.14 | async-start | bytes 1966080 | tf_op jit(solution)/shard_map/all_gather | solution.py:143
  513.8 166.3 %all-reduce.5.cloned.1.call-start = ((), (), s32[]{:S(2)}) async-start(), calls=%async_computation.24 | async-start | bytes 6144000 | tf_op jit(solution)/shard_map/psum | solution.py:312
  516.3 201.7 %reduce-scatter.31.cloned.1.call-start = ((), (), s32[]{:S(2)}) async-start(), calls=%async_computation.29 | async-start | bytes 884736
  519.4 274.0 %reduce-scatter.23.cloned.1.call-start = ((), (), s32[]{:S(2)}) async-start(), calls=%async_computation.23 | async-start | bytes 9437184 | tf_op jit(solution)/shard_map/reduce_scatter | solution.py:331
  558.1 272.7 %reduce-scatter.15.cloned.1.call-start = ((), (), s32[]{:S(2)}) async-start(), calls=%async_computation.15 | async-start | bytes 1966080 | tf_op jit(solution)/shard_map/reduce_scatter | solution.py:146
  565.3 310.8 %reduce-scatter.29.cloned.1.call-start = ((), (), s32[]{:S(2)}) async-start(), calls=%async_computation.28 | async-start | bytes 2654208 | tf_op jit(solution)/shard_map/reduce_scatter | solution.py:330
  571.0 351.8 %reduce-scatter.27.cloned.1.call-start = ((), (), s32[]{:S(2)}) async-start(), calls=%async_computation.27 | async-start | bytes 2654208 | tf_op jit(solution)/shard_map/reduce_scatter | solution.py:329
  575.9 393.1 %reduce-scatter.25.cloned.1.call-start = ((), (), s32[]{:S(2)}) async-start(), calls=%async_computation.26 | async-start | bytes 2654208 | tf_op jit(solution)/shard_map/reduce_scatter | solution.py:327
  580.3 139.3 %copy-start.31 = (f32[768]{0:T(1024)S(1)}, f32[768]{0:T(1024)}, u32[]{:S(2)}) copy-start(f32[768]{0:T(1024)} %get-tuple-element.129) | copy-start | bytes 9220
  580.3 139.3 %copy-start.32 = (f32[768]{0:T(1024)S(1)}, f32[768]{0:T(1024)}, u32[]{:S(2)}) copy-start(f32[768]{0:T(1024)} %get-tuple-element.125) | copy-start | bytes 9220
  580.3 139.3 %copy-start.33 = (f32[768]{0:T(1024)S(1)}, f32[768]{0:T(1024)}, u32[]{:S(2)}) copy-start(f32[768]{0:T(1024)} %get-tuple-element.145) | copy-start | bytes 9220
  580.3 139.3 %copy-start.34 = (f32[768]{0:T(1024)S(1)}, f32[768]{0:T(1024)}, u32[]{:S(2)}) copy-start(f32[768]{0:T(1024)} %get-tuple-element.154) | copy-start | bytes 9220
  580.3 139.4 %copy-start.35 = (f32[768]{0:T(1024)S(1)}, f32[768]{0:T(1024)}, u32[]{:S(2)}) copy-start(f32[768]{0:T(1024)} %get-tuple-element.131) | copy-start | bytes 9220
  580.3 139.4 %copy-start.36 = (f32[768]{0:T(1024)S(1)}, f32[768]{0:T(1024)}, u32[]{:S(2)}) copy-start(f32[768]{0:T(1024)} %get-tuple-element.127) | copy-start | bytes 9220
  580.3 250.5 %copy-start.39 = (f32[768]{0:T(1024)S(1)}, f32[768]{0:T(1024)}, u32[]{:S(2)}) copy-start(f32[768]{0:T(1024)} %param.30) | copy-start | bytes 9220
  580.3 461.3 %all-reduce.7.cloned.1.call-start = ((), (), s32[]{:S(2)}) async-start(), calls=%async_computation.25 | async-start | bytes 6144000 | tf_op jit(solution)/shard_map/psum | solution.py:311
  (34 other events, 257.9 us)
Sparse Core Ops, SparseCore 0:
  50.6 36.1 all-gather.12
  103.5 59.1 reduce-scatter.16
  164.8 37.0 all-gather.10
  204.0 35.9 all-gather.14
  250.5 34.1 reduce-scatter.18
  291.6 36.0 all-gather.16
  349.2 34.1 reduce-scatter.20
  390.7 36.0 all-gather.6
  452.1 59.1 reduce-scatter.12
  513.9 45.5 all-gather.8
  562.5 117.5 all-reduce.4
  684.0 33.9 reduce-scatter.30
  721.8 71.4 reduce-scatter.22
  795.5 35.2 reduce-scatter.14
  834.6 41.4 reduce-scatter.28
  880.2 42.4 reduce-scatter.26
  926.5 42.4 reduce-scatter.24
  972.6 68.9 all-reduce.6
